TPU v7x, 256 devices: a whole 4x4x8 slice. The times are simulated.
256 devices in a mesh: seq: 32 (over z, x_hi, core), ch: 8 (over x_lo, y).
Axes of the slice: x: 4 (x_hi: 2, x_lo: 2; x = x_hi * 2 + x_lo), y: 4, z: 8, core: 2. Of those that a mesh axis runs over, the one named last changes fastest.
Arguments:
- tokens: bfloat16 [2, 65536, 2048], P(None, 'seq', 'ch'), may hold values from -6 to 6
- inner_forward: bfloat16 [512, 512], replicated, may hold values from -0.25 to 0.25
- outer_forward: bfloat16 [128, 128], replicated, may hold values from -0.5 to 0.5
- twiddle_forward: float32 [128, 512], P('seq'), may hold values from 0.5 to 2
- freq_kernel: bfloat16 [128, 512, 2048], P(None, 'seq', 'ch'), may hold values from -6 to 6
- outer_inverse: bfloat16 [128, 128], replicated, may hold values from -0.5 to 0.5
- inner_inverse: bfloat16 [512, 512], replicated, may hold values from -0.25 to 0.25
- twiddle_inverse: float32 [128, 512], P(None, 'seq'), may hold values from 0.5 to 2
- gate_gain: float32 [2048], P('ch'), may hold values from 0.5 to 1.5
- gate_bias: float32 [2048], P('ch'), may hold values from -1 to 1
- norm_gain: float32 [2048], replicated, may hold values from 0.1 to 1.9
- up_weight: bfloat16 [4, 1024, 512], P(None, 'seq'), may hold values from -0.25 to 0.25
- down_weight: bfloat16 [4, 1024, 512], P(None, 'seq'), may hold values from -0.1875 to 0.1875
Outputs:
- layer_out: bfloat16 [2, 65536, 2048], P(None, 'seq', 'ch')
All inputs are finite; a program needn't handle non-finite values.
Results may differ from a plain program's by a relative error of at most 0.008.
Values may be sent and summed in bfloat16 or wider, within the bound.
A program may use at most 128 MiB of HBM per device.

v0:
```python
import jax
import jax.numpy as jnp
from jax import lax
from jax.sharding import PartitionSpec as P


def local(
    tokens,
    inner_forward,
    outer_forward,
    twiddle_forward,
    freq_kernel,
    outer_inverse,
    inner_inverse,
    twiddle_inverse,
    gate_gain,
    gate_bias,
    norm_gain,
    up_weight,
    down_weight,
):
    seq_total, tok_dev, ch_dev = tokens.shape
    inner_size = inner_forward.shape[0]
    outer_dev = tok_dev // inner_size
    blocked = tokens.reshape(seq_total, outer_dev, inner_size, ch_dev)
    section_one = jnp.einsum(
        "kb,xabc->xakc", inner_forward, blocked, preferred_element_type=jnp.float32
    )
    section_one = (section_one * twiddle_forward[None, :, :, None]).astype(jnp.bfloat16)
    spread = lax.all_to_all(section_one, "seq", split_axis=2, concat_axis=1, tiled=True)
    spectrum = jnp.einsum(
        "ka,xabc->xkbc", outer_forward, spread, preferred_element_type=jnp.float32
    )
    spectrum = (spectrum * freq_kernel[None].astype(jnp.float32)).astype(jnp.bfloat16)
    section_two = jnp.einsum(
        "nk,xkbc->xnbc", outer_inverse, spectrum, preferred_element_type=jnp.float32
    )
    section_two = (section_two * twiddle_inverse[None, :, :, None]).astype(jnp.bfloat16)
    gathered = lax.all_to_all(section_two, "seq", split_axis=1, concat_axis=2, tiled=True)
    block_count = up_weight.shape[0]
    width_block = up_weight.shape[2]
    mixed = jnp.einsum("mk,xakc->xamc", inner_inverse, gathered, preferred_element_type=jnp.float32)
    flat = blocked.astype(jnp.float32)
    gate = jax.nn.sigmoid(flat * gate_gain + gate_bias)
    gated = (flat + gate * mixed).astype(jnp.bfloat16)
    full_rows = lax.all_to_all(
        gated.reshape(blocked.shape[0], tok_dev, ch_dev),
        "ch",
        split_axis=1,
        concat_axis=2,
        tiled=True,
    )
    rows_dev = full_rows.shape[1]
    width = full_rows.shape[2]
    rows_f = full_rows.astype(jnp.float32)
    scale = lax.rsqrt(jnp.mean(rows_f * rows_f, axis=-1, keepdims=True) + 1e-06)
    normed = (rows_f * scale * norm_gain).astype(jnp.bfloat16)
    normed_b = normed.reshape(seq_total * rows_dev, block_count, width_block)
    lifted = jnp.einsum(
        "rbi,bji->rbj",
        normed_b,
        lax.all_gather(up_weight, "seq", axis=1, tiled=True),
        preferred_element_type=jnp.float32,
    )
    hidden = jax.nn.gelu(lifted, approximate=True).astype(jnp.bfloat16)
    lowered = jnp.einsum(
        "rbj,bji->rbi",
        hidden,
        lax.all_gather(down_weight, "seq", axis=1, tiled=True),
        preferred_element_type=jnp.float32,
    )
    result_rows = (rows_f + lowered.reshape(seq_total, rows_dev, width)).astype(jnp.bfloat16)
    return lax.all_to_all(result_rows, "ch", split_axis=2, concat_axis=1, tiled=True)


def solution(mesh):
    in_specs = (
        P(None, "seq", "ch"),
        P(),
        P(),
        P("seq", None),
        P(None, "seq", "ch"),
        P(),
        P(),
        P(None, "seq"),
        P("ch"),
        P("ch"),
        P(),
        P(None, "seq", None),
        P(None, "seq", None),
    )
    out_specs = P(None, "seq", "ch")
    return jax.shard_map(local, mesh=mesh, in_specs=in_specs, out_specs=out_specs, check_vma=False)
```

profile of v0, /device:TPU:1, one launch (start us, length us, event | category | flops | bytes accessed | tf_op | source)
XLA Modules:
  0.0 315.9 jit_solution(738062000107273923)
XLA Ops:
  6.5 0.0 copy-start
  6.5 0.7 all-gather.3.cloned.1.call-update
  7.3 0.3 copy-done
  7.6 2.9 fusion.30
  10.5 3.1 copy.90
  13.5 12.6 %all-to-all-start = ((bf16[2,4,512,256]{3,1,0,2:T(4,128)(2,1)}), bf16[2,4,512,256]{3,1,0,2:T(4,128)(2,1)S(1)}, u32[]{:S(2)}, u32[]{:S(2)}) async-start(bf16[2,4,512,256]{3,1,0,2:T(4,128)(2,1)} %copy.90), calls=%async_computation | async-start | bytes 4194304 | tf_op jit(solution)/shard_map/all_to_all | solution.py:30
  26.1 2.9 copy.94
  29.1 55.1 %all-to-all-done = bf16[2,4,512,256]{3,1,0,2:T(4,128)(2,1)S(1)} async-done(((bf16[2,4,512,256]{3,1,0,2:T(4,128)(2,1)}), bf16[2,4,512,256]{3,1,0,2:T(4,128)(2,1)S(1)}, u32[]{:S(2)}, u32[]{:S(2)}) %all-to-all-start) | async-done | bytes 2097184 | tf_op jit(solution)/shard_map/all_to_all | solution.py:30
  84.2 0.4 copy.91
  84.6 1.6 copy.92
  86.3 0.7 copy-done.3
  86.9 4.8 %fusion.15 = bf16[2,128,16,256]{1,3,2,0:T(8,128)(2,1)} fusion(f32[128,16]{0,1:T(8,128)S(1)} %copy-done.7, bf16[2,128,16,256]{3,2,1,0:T(8,128)(2,1)} %bitcast.80, f32[128,16,256]{0,2,1:T(8,128)S(1)} %copy-done.3, bf16[128,128]{1,0:T(8,128)(2,1)S(1)} %copy-done.5, bf16[128,128]{1,0:T(8,128)(2,1)S(1)} %copy-done.6), kind=kOutput, calls=%fused_computation.20 | convolution fusion | flops 541065216 | bytes 6365184 | tf_op jit(solution)/shard_map/nk,xkbc->xnbc/dot_general | solution.py:35
  91.7 4.6 %copy.95 = bf16[2,128,16,256]{3,2,0,1:T(8,128)(2,1)} copy(bf16[2,128,16,256]{1,3,2,0:T(8,128)(2,1)} %fusion.15) | data formatting | bytes 4194304 | tf_op jit(solution)/shard_map/convert_element_type | solution.py:38
  96.3 5.4 %all-to-all-start.1 = ((bf16[2,128,16,256]{3,2,0,1:T(8,128)(2,1)}), bf16[2,128,16,256]{3,2,0,1:T(8,128)(2,1)S(1)}, u32[]{:S(2)}, u32[]{:S(2)}) async-start(bf16[2,128,16,256]{3,2,0,1:T(8,128)(2,1)} %copy.95), calls=%async_computation.1 | async-start | bytes 4194304 | tf_op jit(solution)/shard_map/all_to_all | solution.py:39
  101.8 0.2 all-gather.5.cloned.1.call-start
  102.0 0.5 all-gather.5.cloned.1.call-update
  102.5 0.0 copy-start.9
  102.5 0.0 copy-start.10
  102.5 0.0 copy-start.11
  102.5 4.2 %copy.88 = bf16[2,4,512,256]{2,3,1,0:T(8,128)(2,1)} copy(bf16[2,4,512,256]{3,2,1,0:T(8,128)(2,1)} %bitcast.85) | data formatting | bytes 4194304 | tf_op jit(solution)/shard_map/reshape | solution.py:25
  106.7 49.8 %all-to-all-done.1 = bf16[2,128,16,256]{3,2,0,1:T(8,128)(2,1)S(1)} async-done(((bf16[2,128,16,256]{3,2,0,1:T(8,128)(2,1)}), bf16[2,128,16,256]{3,2,0,1:T(8,128)(2,1)S(1)}, u32[]{:S(2)}, u32[]{:S(2)}) %all-to-all-start.1) | async-done | bytes 2097184 | tf_op jit(solution)/shard_map/all_to_all | solution.py:39
  156.5 0.2 copy.97
  156.7 1.4 copy-done.4
  158.1 4.1 %fusion.19 = bf16[2,4,512,256]{2,3,1,0:T(8,128)(2,1)} fusion(bf16[2,4,512,256]{2,3,1,0:T(8,128)(2,1)S(1)} %copy-done.4, bf16[2,4,512,256]{3,2,1,0:T(8,128)(2,1)S(1)} %bitcast.86, f32[256]{0:T(256)S(1)} %copy-done.10, f32[256]{0:T(256)S(1)} %copy-done.11, bf16[512,512]{1,0:T(8,128)(2,1)S(1)} %copy-done.9), kind=kOutput, calls=%fused_computation.27 | convolution fusion | flops 1083179008 | bytes 6817792 | tf_op jit(solution)/shard_map/mk,xakc->xamc/dot_general | solution.py:42
  162.2 2.8 copy.99
  165.0 0.0 copy-start.8
  165.0 14.0 %copy.100 = bf16[2,2048,256]{2,0,1:T(2,128)(2,1)} copy(bf16[2,2048,256]{2,1,0:T(8,128)(2,1)S(1)} %bitcast.82) | data formatting | bytes 4194304 | tf_op jit(solution)/shard_map/reshape | solution.py:47
  179.0 4.6 %all-to-all-start.2 = ((bf16[2,2048,256]{2,0,1:T(2,128)(2,1)}), bf16[2,2048,256]{2,0,1:T(2,128)(2,1)S(1)}, u32[]{:S(2)}, u32[]{:S(2)}) async-start(bf16[2,2048,256]{2,0,1:T(2,128)(2,1)} %copy.100), calls=%async_computation.2 | async-start | bytes 4194304 | tf_op jit(solution)/shard_map/all_to_all | solution.py:46
  183.6 26.1 %all-to-all-done.2 = bf16[2,2048,256]{2,0,1:T(2,128)(2,1)S(1)} async-done(((bf16[2,2048,256]{2,0,1:T(2,128)(2,1)}), bf16[2,2048,256]{2,0,1:T(2,128)(2,1)S(1)}, u32[]{:S(2)}, u32[]{:S(2)}) %all-to-all-start.2) | async-done | bytes 2097184 | tf_op jit(solution)/shard_map/all_to_all | solution.py:46
  209.7 0.3 copy_convert_fusion
  210.1 1.9 copy-done.2
  212.0 4.4 %copy.103 = f32[2,256,8,256]{3,2,1,0:T(8,128)} copy(f32[2,256,8,256]{3,1,2,0:T(8,128)S(1)} %bitcast.77) | data formatting | bytes 8388608 | tf_op jit(solution)/shard_map/convert_element_type | solution.py:55
  216.4 5.4 %copy.102 = f32[2,256,8,256]{1,3,2,0:T(8,128)} copy(f32[2,256,8,256]{3,1,2,0:T(8,128)} %bitcast.78) | data formatting | bytes 8388608 | tf_op jit(solution)/shard_map/convert_element_type | solution.py:55
  221.8 5.6 %reshape.51 = f32[512,4,512]{2,1,0:T(4,128)} reshape(f32[2,256,8,256]{3,2,1,0:T(8,128)} %copy.103) | data formatting | bytes 8388608 | tf_op jit(solution)/shard_map/convert_element_type | solution.py:55
  227.4 0.6 multiply_reduce_fusion
  228.1 3.4 %multiply_convert_fusion = bf16[512,4,512]{2,1,0:T(4,128)(2,1)S(1)} fusion(f32[512,4,512]{2,1,0:T(4,128)} %reshape.51, f32[4,512]{1,0:T(4,128)S(1)} %mul.95, f32[512]{0:T(512)S(1)} %bitcast.88), kind=kLoop, calls=%fused_computation.23 | loop fusion | flops 3145728 | bytes 6301696 | tf_op jit(solution)/shard_map/convert_element_type | solution.py:57
  231.6 0.0 all-gather.3.cloned.1.call-done
  231.6 0.0 all-gather.5.cloned.1.call-done
  231.6 10.4 %fusion.22 = f32[512,4,512]{2,0,1:T(8,128)} fusion(bf16[4,1024,512]{2,1,0:T(8,128)(2,1)} %all-gather.5.cloned.1.call-done, bf16[4,1024,512]{2,1,0:T(8,128)(2,1)} %all-gather.3.cloned.1.call-done, bf16[512,4,512]{2,1,0:T(4,128)(2,1)S(1)} %multiply_convert_fusion), kind=kOutput, calls=%fused_computation.29 | convolution fusion | flops 4313841664 | bytes 14680064 | tf_op jit(solution)/shard_map/rbj,bji->rbi/dot_general | solution.py:66
  242.0 6.8 %copy.105 = f32[512,4,512]{2,1,0:T(4,128)} copy(f32[512,4,512]{2,0,1:T(8,128)} %fusion.22) | data formatting | bytes 8388608 | tf_op jit(solution)/shard_map/rbj,bji->rbi/transpose | solution.py:66
  248.9 6.1 %reshape.49 = f32[2,256,2048]{2,1,0:T(8,128)} reshape(f32[512,4,512]{2,1,0:T(4,128)} %copy.105) | data formatting | bytes 8388608 | tf_op jit(solution)/shard_map/reshape | solution.py:72
  254.9 5.3 %copy.106 = f32[2,256,2048]{1,2,0:T(8,128)} copy(f32[2,256,2048]{2,1,0:T(8,128)} %reshape.49) | data formatting | bytes 8388608 | tf_op jit(solution)/shard_map/reshape | solution.py:72
  260.3 3.9 %fusion.14 = bf16[2,256,2048]{1,2,0:T(8,128)(2,1)S(1)} fusion(f32[2,256,2048]{1,2,0:T(8,128)} %copy.106, f32[2,256,8,256]{1,3,2,0:T(8,128)} %copy.102), kind=kLoop, calls=%fused_computation.18 | loop fusion | flops 2097152 | bytes 10485760 | tf_op jit(solution)/shard_map/convert_element_type | solution.py:72
  264.2 12.8 %copy.107 = bf16[2,256,2048]{1,0,2:T(2,128)(2,1)S(1)} copy(bf16[2,256,2048]{1,2,0:T(8,128)(2,1)S(1)} %fusion.14) | data formatting | bytes 4194304 | tf_op jit(solution)/shard_map/convert_element_type | solution.py:72
  277.0 0.0 copy-start.1
  277.0 29.4 %all_to_all.63 = bf16[2,256,2048]{1,0,2:T(2,128)(2,1)S(1)} all-to-all(bf16[2,256,2048]{1,0,2:T(2,128)(2,1)S(1)} %copy.107), channel_id=1, replica_groups=mesh['seq'=32,'ch'=8] {'ch'}, dimensions={2} | all-to-all | bytes 4194304 | tf_op jit(solution)/shard_map/all_to_all | solution.py:73
  306.4 0.3 copy.108
  306.7 2.4 copy.109
  (19 shorter events, 0.1 us)
Async XLA Ops:
  6.5 1.0 copy-start
  6.5 225.0 %all-gather.3.cloned.1.call-start = ((), (), s32[]{:S(2)}) async-start(), calls=%async_computation.4 | async-start | bytes 4325376 | tf_op jit(solution)/shard_map/all_gather | solution.py:62
  13.5 70.6 %all-to-all-start = ((bf16[2,4,512,256]{3,1,0,2:T(4,128)(2,1)}), bf16[2,4,512,256]{3,1,0,2:T(4,128)(2,1)S(1)}, u32[]{:S(2)}, u32[]{:S(2)}) async-start(bf16[2,4,512,256]{3,1,0,2:T(4,128)(2,1)} %copy.90), calls=%async_computation | async-start | bytes 4194304 | tf_op jit(solution)/shard_map/all_to_all | solution.py:30
  29.1 57.2 %copy-start.5 = (bf16[128,128]{1,0:T(8,128)(2,1)S(1)}, bf16[128,128]{1,0:T(8,128)(2,1)}, u32[]{:S(2)}) copy-start(bf16[128,128]{1,0:T(8,128)(2,1)} %param.18) | copy-start | bytes 98308
  29.1 57.2 %copy-start.6 = (bf16[128,128]{1,0:T(8,128)(2,1)S(1)}, bf16[128,128]{1,0:T(8,128)(2,1)}, u32[]{:S(2)}) copy-start(bf16[128,128]{1,0:T(8,128)(2,1)} %param.15) | copy-start | bytes 98308
  29.1 57.2 %copy-start.7 = (f32[128,16]{0,1:T(8,128)S(1)}, f32[128,16]{0,1:T(8,128)}, u32[]{:S(2)}) copy-start(f32[128,16]{0,1:T(8,128)} %param.20) | copy-start | bytes 24580
  84.6 2.3 copy-start.3
  96.3 60.2 %all-to-all-start.1 = ((bf16[2,128,16,256]{3,2,0,1:T(8,128)(2,1)}), bf16[2,128,16,256]{3,2,0,1:T(8,128)(2,1)S(1)}, u32[]{:S(2)}, u32[]{:S(2)}) async-start(bf16[2,128,16,256]{3,2,0,1:T(8,128)(2,1)} %copy.95), calls=%async_computation.1 | async-start | bytes 4194304 | tf_op jit(solution)/shard_map/all_to_all | solution.py:39
  101.8 129.9 %all-gather.5.cloned.1.call-start = ((), (), s32[]{:S(2)}) async-start(), calls=%async_computation.5 | async-start | bytes 4325376 | tf_op jit(solution)/shard_map/all_gather | solution.py:69
  102.5 54.2 %copy-start.9 = (bf16[512,512]{1,0:T(8,128)(2,1)S(1)}, bf16[512,512]{1,0:T(8,128)(2,1)}, u32[]{:S(2)}) copy-start(bf16[512,512]{1,0:T(8,128)(2,1)} %param.19) | copy-start | bytes 1572868
  102.5 54.2 %copy-start.10 = (f32[256]{0:T(256)S(1)}, f32[256]{0:T(256)}, u32[]{:S(2)}) copy-start(f32[256]{0:T(256)} %param.22) | copy-start | bytes 3076
  102.5 54.2 %copy-start.11 = (f32[256]{0:T(256)S(1)}, f32[256]{0:T(256)}, u32[]{:S(2)}) copy-start(f32[256]{0:T(256)} %param.21) | copy-start | bytes 3076
  156.5 1.6 copy-start.4
  165.0 18.6 %copy-start.8 = (f32[2048]{0:T(1024)S(1)}, f32[2048]{0:T(1024)}, u32[]{:S(2)}) copy-start(f32[2048]{0:T(1024)} %param.23) | copy-start | bytes 24580
  179.0 30.7 %all-to-all-start.2 = ((bf16[2,2048,256]{2,0,1:T(2,128)(2,1)}), bf16[2,2048,256]{2,0,1:T(2,128)(2,1)S(1)}, u32[]{:S(2)}, u32[]{:S(2)}) async-start(bf16[2,2048,256]{2,0,1:T(2,128)(2,1)} %copy.100), calls=%async_computation.2 | async-start | bytes 4194304 | tf_op jit(solution)/shard_map/all_to_all | solution.py:46
  210.1 2.0 copy-start.2
  277.0 32.0 %copy-start.1 = (bf16[512,512]{1,0:T(8,128)(2,1)S(1)}, bf16[512,512]{1,0:T(8,128)(2,1)}, u32[]{:S(2)}) copy-start(bf16[512,512]{1,0:T(8,128)(2,1)} %param.14) | copy-start | bytes 1572868
Sparse Core Ops, SparseCore 0:
  10.2 102.3 all-gather.2
  115.4 90.0 all-gather.4
where the time goes:
time: 319 us; the launch traced here: 316 us
  waiting for transfers between devices  132 us (41%)
  local copies, waits for them, and re-layouts  87.3 us (27%)
  blocking collectives  29.4 us (9%)
  starting transfers between devices  22.8 us (7%)
  matrix products  22.2 us (7%)
  between operations  13.6 us (4%)
  other arithmetic  8.33 us (3%)
    all_to_all x1, waiting for transfers between devices, local(): lax.all_to_all(section_one, 'seq', split_axis=2, concat_axis=1, tiled=True)  55.1 us
    all_to_all x1, waiting for transfers between devices, local(): lax.all_to_all(section_two, 'seq', split_axis=1, concat_axis=2, tiled=True)  49.8 us
    all_to_all x1, blocking collectives, local(): lax.all_to_all(result_rows, 'ch', split_axis=2, concat_axis=1, tiled=True)  29.4 us
    all_to_all x1, waiting for transfers between devices, local(): lax.all_to_all(gated.reshape(blocked.shape[0], tok_dev, ch_dev), 'ch', sp...  26.1 us
    convert_element_type x3, local copies, waits for them, and re-layouts, local(): rows_f = full_rows.astype(jnp.float32)  15.4 us
    reshape x1, local copies, waits for them, and re-layouts, local(): gated.reshape(blocked.shape[0], tok_dev, ch_dev)  14 us
    convert_element_type x1, local copies, waits for them, and re-layouts, local(): (rows_f + lowered.reshape(seq_total, rows_dev, width)).astype(jnp.bfloat16)  12.8 us
    all_to_all x1, starting transfers between devices, local(): lax.all_to_all(section_one, 'seq', split_axis=2, concat_axis=1, tiled=True)  12.6 us
  transfers between devices with their start and end apart: 5, of which 3 were waited for; matrix products, arithmetic and copies ran while one was open for 21% of the time, Pallas kernels for 0%

commit v1 on v0

v1 whole, which is shorter than its diff:
```python
import functools

import jax
import jax.numpy as jnp
from jax import lax
from jax.experimental import pallas as pl
from jax.experimental.pallas import tpu as pltpu
from jax.sharding import PartitionSpec as P

MESH = pl.DeviceIdType.MESH
BF = jnp.bfloat16
F32 = jnp.float32


def dot(a, b):
    return jnp.dot(a, b, preferred_element_type=F32)


def dot_nt(a, b):
    return lax.dot_general(a, b, (((1,), (1,)), ((), ())), preferred_element_type=F32)


def lanes(col, width):
    return jnp.concatenate([col] * (width // 128), axis=1)


def kernel(
    eps,
    tok, fin, fout, twf, freq, gout, gin, twi, vecs, up, down,
    out,
    x, w_in, w_fo, w_go, w_gi, tw, ti, kraw, vec,
    twb, tib, kt, abuf, bbuf,
    s1, r1, s2, r2, own, other, res, wts, st_own, st_all,
    in_sem, loc_sem, a1_send, a1_recv, a2_send, a2_recv,
    pair_send, pair_recv, st_send, st_recv, wt_send, wt_recv, out_sem,
):
    n_seq, outer_dev = x.shape[0], x.shape[1]
    groups = s1.shape[2]
    kd = s1.shape[3]
    width = x.shape[3]
    inner = x.shape[2]
    outer = fout.shape[0]
    n_ch = st_all.shape[2]
    half = outer_dev // 2

    me = lax.axis_index("seq")
    ch = lax.axis_index("ch")
    z, xh, co = me // 4, (me // 2) % 2, me % 2
    pair = (ch // 2) * 2 + 1 - ch % 2
    block, mine = ch // 2, ch % 2

    loads = [
        pltpu.make_async_copy(tok.at[0], x.at[0], in_sem.at[0]),
        pltpu.make_async_copy(fin, w_in, in_sem.at[1]),
        pltpu.make_async_copy(twf, tw, in_sem.at[2]),
        pltpu.make_async_copy(tok.at[1], x.at[1], in_sem.at[3]),
        pltpu.make_async_copy(fout, w_fo, in_sem.at[4]),
        pltpu.make_async_copy(gout, w_go, in_sem.at[5]),
        pltpu.make_async_copy(gin, w_gi, in_sem.at[6]),
        pltpu.make_async_copy(twi, ti, in_sem.at[7]),
        pltpu.make_async_copy(freq, kraw, in_sem.at[8]),
        pltpu.make_async_copy(vecs, vec, in_sem.at[9]),
        pltpu.make_async_copy(
            up.at[block, :, pl.ds(pl.multiple_of(mine * width, 128), width)],
            wts.at[z, xh, co, 0], in_sem.at[10]),
        pltpu.make_async_copy(
            up.at[block, :, pl.ds(pl.multiple_of((1 - mine) * width, 128), width)],
            wts.at[z, xh, co, 1], in_sem.at[11]),
        pltpu.make_async_copy(
            down.at[block, :, pl.ds(pl.multiple_of(mine * width, 128), width)],
            wts.at[z, xh, co, 2], in_sem.at[12]),
    ]
    for c in loads[10:]:
        c.start()
    for c in loads[:10]:
        c.start()

    bar = pltpu.get_barrier_semaphore()

    def greet_seq(i, _):
        pl.semaphore_signal(bar, inc=1, device_id=((me + i) % groups, ch), device_id_type=MESH)
        return 0

    def greet_ch(i, _):
        pl.semaphore_signal(bar, inc=1, device_id=(me, (ch + i) % n_ch), device_id_type=MESH)
        return 0

    lax.fori_loop(1, groups, greet_seq, 0)
    lax.fori_loop(1, n_ch, greet_ch, 0)

    loads[2].wait()
    for a in range(outer_dev):
        row = jnp.broadcast_to(tw[a : a + 1, :], (128, inner))
        twb[a] = row.T

    pl.semaphore_wait(bar, groups - 1 + n_ch - 1)

    for c in loads[10:]:
        c.wait()

    def weight_to_z(i, _):
        zt = (z + i) % 8
        pltpu.make_async_remote_copy(
            src_ref=wts.at[z, xh, co], dst_ref=wts.at[z, xh, co],
            send_sem=wt_send.at[0], recv_sem=wt_recv.at[0],
            device_id=(zt * 4 + xh * 2 + co, ch), device_id_type=MESH).start()
        return 0

    lax.fori_loop(1, 8, weight_to_z, 0)

    loads[1].wait()
    for s in range(n_seq):
        loads[0 if s == 0 else 3].wait()

        def first(a, _):
            v = dot(w_in[...], x[s, a])
            v = v * lanes(twb[a], width)
            s1[s, a] = v.astype(BF).reshape(groups, kd, width)
            return 0

        lax.fori_loop(0, outer_dev, first, 0)

        def send(i, _):
            j = (me + i) % groups
            pltpu.make_async_remote_copy(
                src_ref=s1.at[s, :, j], dst_ref=r1.at[s, pl.ds(outer_dev * me, outer_dev)],
                send_sem=a1_send.at[s], recv_sem=a1_recv.at[s],
                device_id=(j, ch), device_id_type=MESH).start()
            return 0

        lax.fori_loop(1, groups, send, 0)
        pltpu.make_async_copy(
            s1.at[s, :, me], r1.at[s, pl.ds(outer_dev * me, outer_dev)], loc_sem.at[s]).start()

    side = kd * kd
    ri = lax.broadcasted_iota(jnp.int32, (side, side), 0)
    rj = lax.broadcasted_iota(jnp.int32, (side, side), 1)
    perm = ((ri % kd) * kd + ri // kd == rj).astype(F32).astype(BF)

    def swap(v):
        return dot(perm, v.reshape(side, width)).astype(BF).reshape(kd, kd, width)

    loads[8].wait()

    def prep_kernel(i, _):
        o = pl.multiple_of(i * kd, kd)
        kt[:, pl.ds(o, kd), :] = swap(kraw[pl.ds(o, kd)])
        return 0

    lax.fori_loop(0, outer // kd, prep_kernel, 0)
    loads[7].wait()
    for k in range(kd):
        tib[k] = jnp.broadcast_to(ti[k : k + 1, :], (128, outer)).T

    def line(a, b):
        return wts.at[:, a, b]

    def pull_bytes(count, sem):
        ref = wts.at[pl.ds(0, count), 0, 0]
        pltpu.make_async_copy(ref, ref, sem).wait()

    pull_bytes(7, wt_recv.at[0])
    to_x = pltpu.make_async_remote_copy(
        src_ref=line(xh, co), dst_ref=line(xh, co), send_sem=wt_send.at[1], recv_sem=wt_recv.at[1],
        device_id=(z * 4 + (1 - xh) * 2 + co, ch), device_id_type=MESH)
    to_core = pltpu.make_async_remote_copy(
        src_ref=line(xh, co), dst_ref=line(xh, co), send_sem=wt_send.at[2], recv_sem=wt_recv.at[2],
        device_id=(z * 4 + xh * 2 + 1 - co, ch), device_id_type=MESH)
    relay = pltpu.make_async_remote_copy(
        src_ref=line(1 - xh, co), dst_ref=line(1 - xh, co), send_sem=wt_send.at[3], recv_sem=wt_recv.at[3],
        device_id=(z * 4 + xh * 2 + 1 - co, ch), device_id_type=MESH)
    to_x.start()
    to_core.start()

    loads[4].wait()
    loads[5].wait()

    for s in range(n_seq):
        got = r1.at[s, pl.ds(0, outer - outer_dev)]
        pltpu.make_async_copy(got, got, a1_recv.at[s]).wait()
        pltpu.make_async_copy(
            s1.at[s, :, me], r1.at[s, pl.ds(outer_dev * me, outer_dev)], loc_sem.at[s]).wait()

        def to_k(i, _):
            o = pl.multiple_of(i * kd, kd)
            abuf[:, pl.ds(o, kd), :] = swap(r1[s, pl.ds(o, kd)])
            return 0

        lax.fori_loop(0, outer // kd, to_k, 0)

        def mix(k, _):
            spec = dot(w_fo[...], abuf[k]) * kt[k].astype(F32)
            v = dot(w_go[...], spec.astype(BF)) * lanes(tib[k], width)
            bbuf[k] = v.astype(BF)
            return 0

        lax.fori_loop(0, kd, mix, 0)

        def from_k(i, _):
            o = pl.multiple_of(i * kd, kd)
            s2[s, pl.ds(o, kd)] = swap(bbuf[:, pl.ds(o, kd), :])
            return 0

        lax.fori_loop(0, outer // kd, from_k, 0)

        for h in range(2):
            def send(i, _):
                j = (me + i) % groups
                pltpu.make_async_remote_copy(
                    src_ref=s2.at[s, pl.ds(outer_dev * j + half * h, half)],
                    dst_ref=r2.at[s, pl.ds(half * h, half), me],
                    send_sem=a2_send.at[s, h], recv_sem=a2_recv.at[s, h],
                    device_id=(j, ch), device_id_type=MESH).start()
                return 0

            lax.fori_loop(1, groups, send, 0)
            pltpu.make_async_copy(
                s2.at[s, pl.ds(outer_dev * me + half * h, half)],
                r2.at[s, pl.ds(half * h, half), me], loc_sem.at[n_seq + 2 * s + h]).start()

    to_x.wait_recv()
    relay.start()
    loads[6].wait()
    loads[9].wait()

    def gate(s, h):
        got = r2.at[s, pl.ds(half * h, half), pl.ds(0, groups - 1)]
        pltpu.make_async_copy(got, got, a2_recv.at[s, h]).wait()
        pltpu.make_async_copy(
            s2.at[s, pl.ds(outer_dev * me + half * h, half)],
            r2.at[s, pl.ds(half * h, half), me], loc_sem.at[n_seq + 2 * s + h]).wait()

        def one(n, _):
            mixed = dot(w_gi[...], r2[s, n].reshape(inner, width))
            xf = x[s, n].astype(F32)
            g = jax.nn.sigmoid(xf * vec[0:1, :] + vec[1:2, :])
            y = (xf + g * mixed).astype(BF)
            own[s, n] = y
            pltpu.make_async_remote_copy(
                src_ref=own.at[s, n], dst_ref=other.at[s, n],
                send_sem=pair_send.at[s, n], recv_sem=pair_recv.at[s, n],
                device_id=(me, pair), device_id_type=MESH).start()
            yf = y.astype(F32)
            sq = yf * yf
            part = sq[:, :128]
            for c in range(1, width // 128):
                part = part + sq[:, c * 128 : (c + 1) * 128]
            for b in range(inner // 128):
                t = part[b * 128 : (b + 1) * 128, :].T
                st_own[s, n, :, b * 128 : (b + 1) * 128] = jnp.sum(t, axis=0, keepdims=True)

            def tell(i, _):
                pltpu.make_async_remote_copy(
                    src_ref=st_own.at[s, n], dst_ref=st_all.at[s, n, ch],
                    send_sem=st_send.at[s, n], recv_sem=st_recv.at[s, n],
                    device_id=(me, (ch + i) % n_ch), device_id_type=MESH).start()
                return 0

            lax.fori_loop(1, n_ch, tell, 0)
            st_all[s, n, ch] = st_own[s, n]
            return 0

        lax.fori_loop(half * h, half * (h + 1), one, 0)

    n_q = 4
    zq = 8 // n_q

    def feed(s):
        def one(n, _):
            ref = st_all.at[s, n, pl.ds(0, n_ch - 1)]
            pltpu.make_async_copy(ref, ref, st_recv.at[s, n]).wait()
            total = st_all[s, n, 0]
            for c in range(1, n_ch):
                total = total + st_all[s, n, c]
            scale = lax.rsqrt(total * (1.0 / (n_ch * width)) + eps)
            cols = [
                jnp.broadcast_to(scale[:, b * 128 : (b + 1) * 128], (128, 128)).T
                for b in range(inner // 128)
            ]
            col = lanes(jnp.concatenate(cols, axis=0), width)
            pltpu.make_async_remote_copy(
                src_ref=own.at[s, n], dst_ref=other.at[s, n],
                send_sem=pair_send.at[s, n], recv_sem=pair_recv.at[s, n],
                device_id=(me, pair), device_id_type=MESH).wait()
            yf = own[s, n].astype(F32)
            na = (yf * col * vec[2:3, :]).astype(BF)
            nb = (other[s, n].astype(F32) * col * vec[3:4, :]).astype(BF)
            acc = yf
            for q in range(n_q):
                w = wts[zq * q : zq * (q + 1)]
                rows = zq * 4 * w.shape[4]
                ua = w[:, :, :, 0].reshape(rows, width)
                ub = w[:, :, :, 1].reshape(rows, width)
                dw = w[:, :, :, 2].reshape(rows, width)
                lifted = dot_nt(na, ua) + dot_nt(nb, ub)
                hid = jax.nn.gelu(lifted, approximate=True).astype(BF)
                acc = acc + dot(hid, dw)
            res[s, n] = acc.astype(BF)
            pltpu.make_async_copy(res.at[s, n], out.at[s, n], out_sem).start()
            return 0

        lax.fori_loop(0, outer_dev, one, 0)

    gate(0, 0)
    gate(0, 1)
    to_core.wait_recv()
    relay.wait_recv()
    feed(0)
    gate(1, 0)
    gate(1, 1)
    feed(1)

    pull_bytes(7, wt_send.at[0])
    to_x.wait_send()
    to_core.wait_send()
    relay.wait_send()
    for s in range(n_seq):
        sent = r1.at[s, pl.ds(0, outer - outer_dev)]
        pltpu.make_async_copy(sent, sent, a1_send.at[s]).wait()
        for h in range(2):
            sent = r2.at[s, pl.ds(half * h, half), pl.ds(0, groups - 1)]
            pltpu.make_async_copy(sent, sent, a2_send.at[s, h]).wait()
        for n in range(outer_dev):
            ref = st_all.at[s, n, pl.ds(0, n_ch - 1)]
            pltpu.make_async_copy(ref, ref, st_send.at[s, n]).wait()
    pltpu.make_async_copy(res, out, out_sem).wait()


def local(
    tokens, inner_forward, outer_forward, twiddle_forward, freq_kernel, outer_inverse,
    inner_inverse, twiddle_inverse, gate_gain, gate_bias, norm_gain, up_weight, down_weight,
):
    n_seq, tok_dev, width = tokens.shape
    inner, outer = inner_forward.shape[0], outer_forward.shape[0]
    outer_dev = tok_dev // inner
    groups = outer // outer_dev
    kd = inner // groups
    n_ch = norm_gain.shape[0] // width
    rows = up_weight.shape[1]
    ch = lax.axis_index("ch")
    pair = (ch // 2) * 2 + 1 - ch % 2
    vecs = jnp.stack([
        gate_gain, gate_bias,
        lax.dynamic_slice(norm_gain, (ch * width,), (width,)),
        lax.dynamic_slice(norm_gain, (pair * width,), (width,)),
    ])
    x = tokens.reshape(n_seq, outer_dev, inner, width)
    sems = pltpu.SemaphoreType.DMA
    vm = pltpu.VMEM
    scratch = [
        vm((n_seq, outer_dev, inner, width), BF),
        vm((inner, inner), BF), vm((outer, outer), BF), vm((outer, outer), BF), vm((inner, inner), BF),
        vm((outer_dev, inner), F32), vm((kd, outer), F32), vm((outer, kd, width), BF), vm((4, width), F32),
        vm((outer_dev, inner, 128), F32), vm((kd, outer, 128), F32),
        vm((kd, outer, width), BF), vm((kd, outer, width), BF), vm((kd, outer, width), BF),
        vm((n_seq, outer_dev, groups, kd, width), BF),
        vm((n_seq, outer, kd, width), BF),
        vm((n_seq, outer, kd, width), BF),
        vm((n_seq, outer_dev, groups, kd, width), BF),
        vm((n_seq, outer_dev, inner, width), BF),
        vm((n_seq, outer_dev, inner, width), BF),
        vm((n_seq, outer_dev, inner, width), BF),
        vm((8, 2, 2, 3, rows, width), BF),
        vm((n_seq, outer_dev, 1, inner), F32),
        vm((n_seq, outer_dev, n_ch, 1, inner), F32),
        sems((13,)), sems((3 * n_seq,)),
        sems((n_seq,)), sems((n_seq,)), sems((n_seq, 2)), sems((n_seq, 2)),
        sems((n_seq, outer_dev)), sems((n_seq, outer_dev)),
        sems((n_seq, outer_dev)), sems((n_seq, outer_dev)),
        sems((4,)), sems((4,)), sems,
    ]
    any_spec = pl.BlockSpec(memory_space=pl.ANY)
    y = pl.pallas_call(
        functools.partial(kernel, 1e-06),
        out_shape=jax.ShapeDtypeStruct((n_seq, outer_dev, inner, width), BF),
        in_specs=[any_spec] * 11,
        out_specs=any_spec,
        scratch_shapes=scratch,
        compiler_params=pltpu.CompilerParams(
            collective_id=0, has_side_effects=True, vmem_limit_bytes=60 * 1024 * 1024),
        name="mixer",
    )(
        x, inner_forward, outer_forward, twiddle_forward, freq_kernel, outer_inverse,
        inner_inverse, twiddle_inverse.T, vecs, up_weight, down_weight,
    )
    return y.reshape(n_seq, tok_dev, width)


def solution(mesh):
    in_specs = (
        P(None, "seq", "ch"),
        P(),
        P(),
        P("seq", None),
        P(None, "seq", "ch"),
        P(),
        P(),
        P(None, "seq"),
        P("ch"),
        P("ch"),
        P(),
        P(None, "seq", None),
        P(None, "seq", None),
    )
    out_specs = P(None, "seq", "ch")
    return jax.shard_map(local, mesh=mesh, in_specs=in_specs, out_specs=out_specs, check_vma=False)
```

time: 319 us -> 141 us (0.44)
  Pallas kernels: 0 us -> 135 us
  waiting for transfers between devices: 132 us -> 0 us
  local copies, waits for them, and re-layouts: 87.3 us -> 3.88 us
  blocking collectives: 29.4 us -> 0 us
  starting transfers between devices: 22.8 us -> 0 us
  matrix products: 22.2 us -> 0 us
  between operations: 13.6 us -> 0.01 us
  other arithmetic: 8.33 us -> 1.3 us
    pallas_call x0 -> x1, Pallas kernels: none -> 135 us  [local(): pl.pallas_call(functools.partial(kernel, 1e-06), out_shape=jax.ShapeDtype...]
    all_to_all x3 -> x0, waiting for transfers between devices: 131 us -> none  [the longest x1 55.1 us: local(): lax.all_to_all(section_one, 'seq', split_axis=2, concat_axis=1, tiled=True)]
    convert_element_type x8 -> x0, local copies, waits for them, and re-layouts: 41.6 us -> none  [the longest x3 15.4 us: local(): rows_f = full_rows.astype(jnp.float32)]
    reshape x4 -> x0, local copies, waits for them, and re-layouts: 29.6 us -> none  [the longest x1 14 us: local(): gated.reshape(blocked.shape[0], tok_dev, ch_dev)]
    all_to_all x1 -> x0, blocking collectives: 29.4 us -> none  [local(): lax.all_to_all(result_rows, 'ch', split_axis=2, concat_axis=1, tiled=True)]
    all_to_all x3 -> x0, starting transfers between devices: 22.6 us -> none  [the longest x1 12.6 us: local(): lax.all_to_all(section_one, 'seq', split_axis=2, concat_axis=1, tiled=True)]
    dot_general x4 -> x0, matrix products: 22.2 us -> none  [the longest x1 10.4 us: local(): jnp.einsum('rbj,bji->rbi', hidden, lax.all_gather(down_weight, 'seq', axi...]
    convert_element_type x3 -> x0, other arithmetic: 7.67 us -> none  [the longest x1 3.91 us: local(): (rows_f + lowered.reshape(seq_total, rows_dev, width)).astype(jnp.bfloat16)]
  transfers between devices with their start and end apart: 5 -> 0, of which waited for: 3 -> 0; matrix products, arithmetic and copies ran while one was open for 21% -> 0% of each run, Pallas kernels for 0% -> 0%
where the time goes in v1:
time: 141 us; the launch traced here: 140 us
  Pallas kernels  135 us (96%)
  local copies, waits for them, and re-layouts  3.88 us (3%)
    pallas_call x1, Pallas kernels, local(): pl.pallas_call(functools.partial(kernel, 1e-06), out_shape=jax.ShapeDtype...  135 us
    unnamed x1, local copies, waits for them, and re-layouts  3.05 us

profile of v1, /device:TPU:1, one launch (start us, length us, event | category | flops | bytes accessed | tf_op | source)
XLA Modules:
  0.0 140.5 jit_solution(14821700547641498074)
XLA Ops:
  0.0 0.8 fusion
  0.8 1.3 pad_maximum_fusion.vecs
  2.1 135.3 %mixer.1 = bf16[2,4,512,256]{3,2,1,0:T(8,128)(2,1)} custom-call(bf16[2,4,512,256]{3,2,1,0:T(8,128)(2,1)} %bitcast.8, bf16[512,512]{1,0:T(8,128)(2,1)} %fin.1, bf16[128,128]{1,0:T(8,128)(2,1)} %fout.1, f32[4,512]{1,0:T(4,128)} %twf.1, bf16[128,16,256]{2,1,0:T(8,128)(2,1)} %freq.1, bf16[128,128]{1,0:T(8,128)(2,1)} %gout.1, bf16[512,512]{1,0:T(8,128)(2,1)} %gin.1, ...), custom_call_target="tpu_custom_call" | custom-call | tf_op jit(solution)/shard_map/mixer/pallas_call | solution.py:373
  137.4 3.0 %copy.15 = bf16[2,2048,256]{2,1,0:T(8,128)(2,1)} copy(bf16[2,2048,256]{2,1,0:T(8,128)(2,1)} %bitcast.7) | data formatting | bytes 4194304

commit v2 on v1

v2 whole, which is shorter than its diff:
```python
import functools

import jax
import jax.numpy as jnp
from jax import lax
from jax.experimental import pallas as pl
from jax.experimental.pallas import tpu as pltpu
from jax.sharding import PartitionSpec as P

MESH = pl.DeviceIdType.MESH
BF = jnp.bfloat16
F32 = jnp.float32


def dot(a, b):
    return jnp.dot(a, b, preferred_element_type=F32)


def dot_nt(a, b):
    return lax.dot_general(a, b, (((1,), (1,)), ((), ())), preferred_element_type=F32)


def lanes(col, width):
    return jnp.concatenate([col] * (width // 128), axis=1)


def kernel(
    eps,
    tok, fin, fout, twf, freq, gout, gin, twi, gain, bias, norm, up, down,
    out,
    x, w_in, w_fo, w_go, w_gi, tw, ti, kraw, vec,
    twb, tib, kt, abuf, bbuf,
    s1, r1, s2, r2, own, other, wts, st_own, st_all,
    in_sem, loc_sem, loc2_sem, a1_send, a1_recv, a2_send, a2_recv,
    pair_send, pair_recv, st_send, st_recv, wt_send, wt_recv,
):
    n_seq, outer_dev = x.shape[0], x.shape[1]
    groups = s1.shape[2]
    kd = s1.shape[3]
    width = x.shape[3]
    inner = x.shape[2]
    outer = fout.shape[0]
    n_ch = st_all.shape[2]

    me = lax.axis_index("seq")
    ch = lax.axis_index("ch")
    z, xh, co = me // 4, (me // 2) % 2, me % 2
    pair = (ch // 2) * 2 + 1 - ch % 2
    block, mine = ch // 2, ch % 2

    loads = [
        pltpu.make_async_copy(tok.at[0], x.at[0], in_sem.at[0]),
        pltpu.make_async_copy(fin, w_in, in_sem.at[1]),
        pltpu.make_async_copy(twf, tw, in_sem.at[2]),
        pltpu.make_async_copy(tok.at[1], x.at[1], in_sem.at[3]),
        pltpu.make_async_copy(fout, w_fo, in_sem.at[4]),
        pltpu.make_async_copy(gout, w_go, in_sem.at[5]),
        pltpu.make_async_copy(gin, w_gi, in_sem.at[6]),
        pltpu.make_async_copy(twi, ti, in_sem.at[7]),
        pltpu.make_async_copy(freq, kraw, in_sem.at[8]),
        pltpu.make_async_copy(gain, vec.at[0], in_sem.at[9]),
        pltpu.make_async_copy(bias, vec.at[1], in_sem.at[10]),
        pltpu.make_async_copy(norm.at[ch], vec.at[2], in_sem.at[11]),
        pltpu.make_async_copy(norm.at[pair], vec.at[3], in_sem.at[12]),
    ]
    cols = pl.ds(pl.multiple_of(mine * width, 128), width)
    shard = [
        pltpu.make_async_copy(up.at[block, :, cols], wts.at[z, xh, co, 0], in_sem.at[13]),
        pltpu.make_async_copy(down.at[block, :, cols], wts.at[z, xh, co, 1], in_sem.at[14]),
    ]
    for c in loads[:3] + shard + loads[3:]:
        c.start()

    bar = pltpu.get_barrier_semaphore()

    def greet_seq(i, _):
        pl.semaphore_signal(bar, inc=1, device_id=((me + i) % groups, ch), device_id_type=MESH)
        return 0

    def greet_ch(i, _):
        pl.semaphore_signal(bar, inc=1, device_id=(me, (ch + i) % n_ch), device_id_type=MESH)
        return 0

    lax.fori_loop(1, groups, greet_seq, 0)
    lax.fori_loop(1, n_ch, greet_ch, 0)

    loads[2].wait()
    for a in range(outer_dev):
        row = jnp.broadcast_to(tw[a : a + 1, :], (128, inner))
        twb[a] = row.T

    turn = 1 - 2 * co

    def piece(dz):
        return wts.at[(z + dz + 8) % 8, xh, co, pl.ds(0, 2)]

    def to_z(src, dz, k):
        return pltpu.make_async_remote_copy(
            src_ref=piece(src), dst_ref=piece(src), send_sem=wt_send.at[k], recv_sem=wt_recv.at[k],
            device_id=((z + dz + 8) % 8 * 4 + xh * 2 + co, ch), device_id_type=MESH)

    direct = [to_z(0, turn, 0), to_z(0, -turn, 1), to_z(0, 2 * turn, 2), to_z(0, -2 * turn, 3)]
    passed = [to_z(-2 * turn, turn, 4), to_z(-2 * turn, 2 * turn, 5), to_z(2 * turn, -turn, 6)]

    loads[1].wait()
    for s in range(n_seq):
        loads[0 if s == 0 else 3].wait()

        def first(a, _):
            v = dot(w_in[...], x[s, a])
            v = v * lanes(twb[a], width)
            s1[s, a] = v.astype(BF).reshape(groups, kd, width)
            return 0

        lax.fori_loop(0, outer_dev, first, 0)
        if s == 0:
            pl.semaphore_wait(bar, groups - 1 + n_ch - 1)
            for c in shard:
                c.wait()
            for c in direct:
                c.start()

        def send(i, _):
            j = (me + i) % groups
            pltpu.make_async_remote_copy(
                src_ref=s1.at[s, :, j], dst_ref=r1.at[s, pl.ds(outer_dev * me, outer_dev)],
                send_sem=a1_send.at[s], recv_sem=a1_recv.at[s],
                device_id=(j, ch), device_id_type=MESH).start()
            return 0

        lax.fori_loop(1, groups, send, 0)
        pltpu.make_async_copy(
            s1.at[s, :, me], r1.at[s, pl.ds(outer_dev * me, outer_dev)], loc_sem.at[s]).start()
        if s == 0:
            direct[2].wait_recv()
            passed[0].start()
            passed[1].start()
            direct[3].wait_recv()
            passed[2].start()

    side = kd * kd
    ri = lax.broadcasted_iota(jnp.int32, (side, side), 0)
    rj = lax.broadcasted_iota(jnp.int32, (side, side), 1)
    perm = ((ri % kd) * kd + ri // kd == rj).astype(F32).astype(BF)

    def swap(v):
        return dot(perm, v.reshape(side, width)).astype(BF).reshape(kd, kd, width)

    loads[8].wait()

    def prep_kernel(i, _):
        o = pl.multiple_of(i * kd, kd)
        kt[:, pl.ds(o, kd), :] = swap(kraw[pl.ds(o, kd)])
        return 0

    lax.fori_loop(0, outer // kd, prep_kernel, 0)
    loads[7].wait()
    for k in range(kd):
        tib[k] = jnp.broadcast_to(ti[k : k + 1, :], (128, outer)).T

    def line(a, b):
        return wts.at[:, a, b]

    to_y = pltpu.make_async_remote_copy(
        src_ref=wts.at[:, xh, co, 0], dst_ref=wts.at[:, xh, co, 2],
        send_sem=wt_send.at[7], recv_sem=wt_recv.at[7],
        device_id=(me, pair), device_id_type=MESH)
    to_x = pltpu.make_async_remote_copy(
        src_ref=line(xh, co), dst_ref=line(xh, co), send_sem=wt_send.at[8], recv_sem=wt_recv.at[8],
        device_id=(z * 4 + (1 - xh) * 2 + co, ch), device_id_type=MESH)
    to_core = pltpu.make_async_remote_copy(
        src_ref=line(xh, co), dst_ref=line(xh, co), send_sem=wt_send.at[9], recv_sem=wt_recv.at[9],
        device_id=(z * 4 + xh * 2 + 1 - co, ch), device_id_type=MESH)
    relay = pltpu.make_async_remote_copy(
        src_ref=line(1 - xh, co), dst_ref=line(1 - xh, co), send_sem=wt_send.at[10], recv_sem=wt_recv.at[10],
        device_id=(z * 4 + xh * 2 + 1 - co, ch), device_id_type=MESH)
    for c in direct[:2] + passed:
        c.wait_recv()
    to_y.start()

    loads[4].wait()
    loads[5].wait()

    def keep(s, n):
        return pltpu.make_async_copy(s2.at[s, outer_dev * me + n], r2.at[s, n, me], loc2_sem.at[s, n])

    for s in range(n_seq):
        got = r1.at[s, pl.ds(0, outer - outer_dev)]
        pltpu.make_async_copy(got, got, a1_recv.at[s]).wait()
        pltpu.make_async_copy(
            s1.at[s, :, me], r1.at[s, pl.ds(outer_dev * me, outer_dev)], loc_sem.at[s]).wait()

        def to_k(i, _):
            o = pl.multiple_of(i * kd, kd)
            abuf[:, pl.ds(o, kd), :] = swap(r1[s, pl.ds(o, kd)])
            return 0

        lax.fori_loop(0, outer // kd, to_k, 0)

        def mix(k, _):
            spec = dot(w_fo[...], abuf[k]) * kt[k].astype(F32)
            v = dot(w_go[...], spec.astype(BF)) * lanes(tib[k], width)
            bbuf[k] = v.astype(BF)
            return 0

        lax.fori_loop(0, kd, mix, 0)

        def from_k(i, _):
            o = pl.multiple_of(i * kd, kd)
            s2[s, pl.ds(o, kd)] = swap(bbuf[:, pl.ds(o, kd), :])
            return 0

        lax.fori_loop(0, outer // kd, from_k, 0)

        def send_row(n, _):
            def send(i, _):
                j = (me + i) % groups
                pltpu.make_async_remote_copy(
                    src_ref=s2.at[s, outer_dev * j + n], dst_ref=r2.at[s, n, me],
                    send_sem=a2_send.at[s, n], recv_sem=a2_recv.at[s, n],
                    device_id=(j, ch), device_id_type=MESH).start()
                return 0

            lax.fori_loop(1, groups, send, 0)
            keep(s, n).start()
            return 0

        lax.fori_loop(0, outer_dev, send_row, 0)
        if s == 0:
            to_y.wait_recv()
            to_x.start()
            to_core.start()

    to_x.wait_recv()
    relay.start()
    loads[6].wait()
    for c in loads[9:]:
        c.wait()

    half = inner // 2

    def to_pair(s, n, r):
        rows = pl.ds(r * half, half)
        return pltpu.make_async_remote_copy(
            src_ref=own.at[s, n, rows], dst_ref=other.at[s, n, rows],
            send_sem=pair_send.at[s, n, r], recv_sem=pair_recv.at[s, n, r],
            device_id=(me, pair), device_id_type=MESH)

    def gate(s, n):
        got = r2.at[s, n, pl.ds(0, groups - 1)]
        pltpu.make_async_copy(got, got, a2_recv.at[s, n]).wait()
        keep(s, n).wait()
        sec = r2[s, n].reshape(inner, width)
        for r in range(2):
            rows = slice(r * half, (r + 1) * half)
            mixed = dot(w_gi[rows, :], sec)
            xf = x[s, n, rows].astype(F32)
            g = jax.nn.sigmoid(xf * vec[0] + vec[1])
            y = (xf + g * mixed).astype(BF)
            own[s, n, rows] = y
            yf = y.astype(F32)
            sq = yf * yf
            part = sq[:, :128]
            for c in range(1, width // 128):
                part = part + sq[:, c * 128 : (c + 1) * 128]
            for b in range(half // 128):
                t = part[b * 128 : (b + 1) * 128, :].T
                at = r * half + b * 128
                st_own[s, n, :, at : at + 128] = jnp.sum(t, axis=0, keepdims=True)
            if r == 0:
                to_pair(s, n, 0).start()

        def tell(i, _):
            pltpu.make_async_remote_copy(
                src_ref=st_own.at[s, n], dst_ref=st_all.at[s, n, ch],
                send_sem=st_send.at[s, n], recv_sem=st_recv.at[s, n],
                device_id=(me, (ch + i) % n_ch), device_id_type=MESH).start()
            return 0

        lax.fori_loop(1, n_ch, tell, 0)
        to_pair(s, n, 1).start()
        st_all[s, n, ch] = st_own[s, n]

    n_q = 4
    zq = 8 // n_q

    def feed(s, n):
        ref = st_all.at[s, n, pl.ds(0, n_ch - 1)]
        pltpu.make_async_copy(ref, ref, st_recv.at[s, n]).wait()
        total = st_all[s, n, 0]
        for c in range(1, n_ch):
            total = total + st_all[s, n, c]
        scale = lax.rsqrt(total * (1.0 / (n_ch * width)) + eps)
        for r in range(2):
            rows = slice(r * half, (r + 1) * half)
            cols = [
                jnp.broadcast_to(scale[:, r * half + b * 128 : r * half + (b + 1) * 128], (128, 128)).T
                for b in range(half // 128)
            ]
            col = lanes(jnp.concatenate(cols, axis=0), width)
            to_pair(s, n, r).wait()
            yf = own[s, n, rows].astype(F32)
            na = (yf * col * vec[2]).astype(BF)
            nb = (other[s, n, rows].astype(F32) * col * vec[3]).astype(BF)
            acc = yf
            for q in range(n_q):
                w = wts[zq * q : zq * (q + 1)]
                depth = zq * 4 * w.shape[4]
                ua = w[:, :, :, 0].reshape(depth, width)
                ub = w[:, :, :, 2].reshape(depth, width)
                dw = w[:, :, :, 1].reshape(depth, width)
                lifted = dot_nt(na, ua) + dot_nt(nb, ub)
                hid = jax.nn.gelu(lifted, approximate=True).astype(BF)
                acc = acc + dot(hid, dw)
            out[s, n, rows] = acc.astype(BF)

    gate(0, 0)
    to_core.wait_recv()
    relay.wait_recv()

    def step(t, _):
        gate(t // outer_dev, t % outer_dev)
        feed((t - 1) // outer_dev, (t - 1) % outer_dev)
        return 0

    lax.fori_loop(1, n_seq * outer_dev, step, 0)
    feed(n_seq - 1, outer_dev - 1)

    for c in direct + passed + [to_y, to_x, to_core, relay]:
        c.wait_send()
    for s in range(n_seq):
        sent = r1.at[s, pl.ds(0, outer - outer_dev)]
        pltpu.make_async_copy(sent, sent, a1_send.at[s]).wait()
        for n in range(outer_dev):
            ref = st_all.at[s, n, pl.ds(0, n_ch - 1)]
            pltpu.make_async_copy(ref, ref, st_send.at[s, n]).wait()
            sent = r2.at[s, n, pl.ds(0, groups - 1)]
            pltpu.make_async_copy(sent, sent, a2_send.at[s, n]).wait()


def local(
    tokens, inner_forward, outer_forward, twiddle_forward, freq_kernel, outer_inverse,
    inner_inverse, twiddle_inverse, gate_gain, gate_bias, norm_gain, up_weight, down_weight,
):
    n_seq, tok_dev, width = tokens.shape
    inner, outer = inner_forward.shape[0], outer_forward.shape[0]
    outer_dev = tok_dev // inner
    groups = outer // outer_dev
    kd = inner // groups
    n_ch = norm_gain.shape[0] // width
    rows = up_weight.shape[1]
    x = tokens.reshape(n_seq, outer_dev, inner, width)
    sems = pltpu.SemaphoreType.DMA
    vm = pltpu.VMEM
    scratch = [
        vm((n_seq, outer_dev, inner, width), BF),
        vm((inner, inner), BF), vm((outer, outer), BF), vm((outer, outer), BF), vm((inner, inner), BF),
        vm((outer_dev, inner), F32), vm((kd, outer), F32), vm((outer, kd, width), BF), vm((4, 1, width), F32),
        vm((outer_dev, inner, 128), F32), vm((kd, outer, 128), F32),
        vm((kd, outer, width), BF), vm((kd, outer, width), BF), vm((kd, outer, width), BF),
        vm((n_seq, outer_dev, groups, kd, width), BF),
        vm((n_seq, outer, kd, width), BF),
        vm((n_seq, outer, kd, width), BF),
        vm((n_seq, outer_dev, groups, kd, width), BF),
        vm((n_seq, outer_dev, inner, width), BF),
        vm((n_seq, outer_dev, inner, width), BF),
        vm((8, 2, 2, 3, rows, width), BF),
        vm((n_seq, outer_dev, 1, inner), F32),
        vm((n_seq, outer_dev, n_ch, 1, inner), F32),
        sems((15,)), sems((n_seq,)), sems((n_seq, outer_dev)),
        sems((n_seq,)), sems((n_seq,)), sems((n_seq, outer_dev)), sems((n_seq, outer_dev)),
        sems((n_seq, outer_dev, 2)), sems((n_seq, outer_dev, 2)),
        sems((n_seq, outer_dev)), sems((n_seq, outer_dev)),
        sems((11,)), sems((11,)),
    ]
    y = pl.pallas_call(
        functools.partial(kernel, 1e-06),
        out_shape=jax.ShapeDtypeStruct((n_seq, outer_dev, inner, width), BF),
        in_specs=[pl.BlockSpec(memory_space=pltpu.HBM)] * 13,
        out_specs=pl.BlockSpec(memory_space=pltpu.VMEM),
        scratch_shapes=scratch,
        compiler_params=pltpu.CompilerParams(
            collective_id=0, has_side_effects=True, vmem_limit_bytes=48 * 1024 * 1024),
        name="mixer",
    )(*[pltpu.with_memory_space_constraint(a, pltpu.HBM) for a in (
        x, inner_forward, outer_forward, twiddle_forward, freq_kernel, outer_inverse,
        inner_inverse, twiddle_inverse.T, gate_gain.reshape(1, width), gate_bias.reshape(1, width),
        norm_gain.reshape(n_ch, 1, width), up_weight, down_weight,
    )])
    return y.reshape(n_seq, tok_dev, width)


def solution(mesh):
    in_specs = (
        P(None, "seq", "ch"),
        P(),
        P(),
        P("seq", None),
        P(None, "seq", "ch"),
        P(),
        P(),
        P(None, "seq"),
        P("ch"),
        P("ch"),
        P(),
        P(None, "seq", None),
        P(None, "seq", None),
    )
    out_specs = P(None, "seq", "ch")
    return jax.shard_map(local, mesh=mesh, in_specs=in_specs, out_specs=out_specs, check_vma=False)
```

time: 141 us -> 124 us (0.88)
  Pallas kernels: 135 us -> 123 us
  local copies, waits for them, and re-layouts: 3.88 us -> 1.32 us
    pallas_call x1, Pallas kernels: 135 us -> 123 us  [local(): pl.pallas_call(functools.partial(kernel, 1e-06), out_shape=jax.ShapeDtype...]
    unnamed x1, local copies, waits for them, and re-layouts: 3.05 us -> 1.32 us
where the time goes in v2:
time: 124 us
  Pallas kernels  123 us (99%)
  local copies, waits for them, and re-layouts  1.32 us (1%)
    pallas_call x1, Pallas kernels, local(): pl.pallas_call(functools.partial(kernel, 1e-06), out_shape=jax.ShapeDtype...  123 us

profile of v2, /device:TPU:1, one launch (start us, length us, event | category | flops | bytes accessed | tf_op | source)
XLA Modules:
  0.0 123.8 jit_solution(18419510185062092873)
XLA Ops:
  0.0 122.5 %mixer.1 = bf16[2,4,512,256]{3,2,1,0:T(8,128)(2,1)S(1)} custom-call(bf16[2,4,512,256]{3,2,1,0:T(8,128)(2,1)} %bitcast.7, bf16[512,512]{1,0:T(8,128)(2,1)} %fin.1, bf16[128,128]{1,0:T(8,128)(2,1)} %fout.1, f32[4,512]{1,0:T(4,128)} %twf.1, bf16[128,16,256]{2,1,0:T(8,128)(2,1)} %freq.1, bf16[128,128]{1,0:T(8,128)(2,1)} %gout.1, bf16[512,512]{1,0:T(8,128)(2,1)} %gin.1, ...), custom_call_target="tpu_custom_call" | custom-call | tf_op jit(solution)/shard_map/mixer/pallas_call | solution.py:376
  122.5 1.3 %copy.15 = bf16[2,2048,256]{2,1,0:T(8,128)(2,1)} copy(bf16[2,2048,256]{2,1,0:T(8,128)(2,1)S(1)} %bitcast.6) | data formatting | bytes 4194304

commit v3 on v2

--- a/solution.py
+++ b/solution.py
@@ -68,7 +68,7 @@
         pltpu.make_async_copy(up.at[block, :, cols], wts.at[z, xh, co, 0], in_sem.at[13]),
         pltpu.make_async_copy(down.at[block, :, cols], wts.at[z, xh, co, 1], in_sem.at[14]),
     ]
-    for c in loads[:3] + shard + loads[3:]:
+    for c in loads[:3]:
         c.start()
 
     bar = pltpu.get_barrier_semaphore()
@@ -83,11 +83,8 @@
 
     lax.fori_loop(1, groups, greet_seq, 0)
     lax.fori_loop(1, n_ch, greet_ch, 0)
-
-    loads[2].wait()
-    for a in range(outer_dev):
-        row = jnp.broadcast_to(tw[a : a + 1, :], (128, inner))
-        twb[a] = row.T
+    for c in shard + loads[3:]:
+        c.start()
 
     turn = 1 - 2 * co
 
@@ -101,6 +98,19 @@
 
     direct = [to_z(0, turn, 0), to_z(0, -turn, 1), to_z(0, 2 * turn, 2), to_z(0, -2 * turn, 3)]
     passed = [to_z(-2 * turn, turn, 4), to_z(-2 * turn, 2 * turn, 5), to_z(2 * turn, -turn, 6)]
+
+    early = outer_dev // 2
+
+    def send_one(s, lo, size):
+        def send(i, _):
+            j = (me + i) % groups
+            pltpu.make_async_remote_copy(
+                src_ref=s1.at[s, pl.ds(lo, size), j], dst_ref=r1.at[s, pl.ds(outer_dev * me + lo, size)],
+                send_sem=a1_send.at[s], recv_sem=a1_recv.at[s],
+                device_id=(j, ch), device_id_type=MESH).start()
+            return 0
+
+        lax.fori_loop(1, groups, send, 0)
 
     loads[1].wait()
     for s in range(n_seq):
@@ -112,23 +122,22 @@
             s1[s, a] = v.astype(BF).reshape(groups, kd, width)
             return 0
 
-        lax.fori_loop(0, outer_dev, first, 0)
         if s == 0:
-            pl.semaphore_wait(bar, groups - 1 + n_ch - 1)
-            for c in shard:
-                c.wait()
-            for c in direct:
-                c.start()
-
-        def send(i, _):
-            j = (me + i) % groups
-            pltpu.make_async_remote_copy(
-                src_ref=s1.at[s, :, j], dst_ref=r1.at[s, pl.ds(outer_dev * me, outer_dev)],
-                send_sem=a1_send.at[s], recv_sem=a1_recv.at[s],
-                device_id=(j, ch), device_id_type=MESH).start()
-            return 0
-
-        lax.fori_loop(1, groups, send, 0)
+            loads[2].wait()
+            for a in range(outer_dev):
+                twb[a] = jnp.broadcast_to(tw[a : a + 1, :], (128, inner)).T
+                first(a, 0)
+                if a == early - 1:
+                    pl.semaphore_wait(bar, groups - 1 + n_ch - 1)
+                    for c in shard:
+                        c.wait()
+                    for c in direct:
+                        c.start()
+                    send_one(0, 0, early)
+            send_one(0, early, outer_dev - early)
+        else:
+            lax.fori_loop(0, outer_dev, first, 0)
+            send_one(s, 0, early)
         pltpu.make_async_copy(
             s1.at[s, :, me], r1.at[s, pl.ds(outer_dev * me, outer_dev)], loc_sem.at[s]).start()
         if s == 0:
@@ -184,34 +193,31 @@
     def keep(s, n):
         return pltpu.make_async_copy(s2.at[s, outer_dev * me + n], r2.at[s, n, me], loc2_sem.at[s, n])
 
-    for s in range(n_seq):
+    unroll = 8
+
+    def middle(s):
         got = r1.at[s, pl.ds(0, outer - outer_dev)]
         pltpu.make_async_copy(got, got, a1_recv.at[s]).wait()
         pltpu.make_async_copy(
             s1.at[s, :, me], r1.at[s, pl.ds(outer_dev * me, outer_dev)], loc_sem.at[s]).wait()
 
-        def to_k(i, _):
-            o = pl.multiple_of(i * kd, kd)
-            abuf[:, pl.ds(o, kd), :] = swap(r1[s, pl.ds(o, kd)])
+        for o in range(0, outer, kd):
+            abuf[:, o : o + kd, :] = swap(r1[s, o : o + kd])
+
+        def mix(i, _):
+            ks = [i * unroll + q for q in range(unroll)]
+            spec = [(dot(w_fo[...], abuf[k]) * kt[k].astype(F32)).astype(BF) for k in ks]
+            for k, v in zip(ks, spec):
+                bbuf[k] = (dot(w_go[...], v) * lanes(tib[k], width)).astype(BF)
             return 0
 
-        lax.fori_loop(0, outer // kd, to_k, 0)
-
-        def mix(k, _):
-            spec = dot(w_fo[...], abuf[k]) * kt[k].astype(F32)
-            v = dot(w_go[...], spec.astype(BF)) * lanes(tib[k], width)
-            bbuf[k] = v.astype(BF)
-            return 0
-
-        lax.fori_loop(0, kd, mix, 0)
-
-        def from_k(i, _):
-            o = pl.multiple_of(i * kd, kd)
-            s2[s, pl.ds(o, kd)] = swap(bbuf[:, pl.ds(o, kd), :])
-            return 0
-
-        lax.fori_loop(0, outer // kd, from_k, 0)
-
+        lax.fori_loop(0, kd // unroll, mix, 0)
+
+        for o in range(0, outer, kd):
+            s2[s, o : o + kd] = swap(bbuf[:, o : o + kd, :])
+
+
+    def send_two(s, lo, hi):
         def send_row(n, _):
             def send(i, _):
                 j = (me + i) % groups
@@ -225,17 +231,7 @@
             keep(s, n).start()
             return 0
 
-        lax.fori_loop(0, outer_dev, send_row, 0)
-        if s == 0:
-            to_y.wait_recv()
-            to_x.start()
-            to_core.start()
-
-    to_x.wait_recv()
-    relay.start()
-    loads[6].wait()
-    for c in loads[9:]:
-        c.wait()
+        lax.fori_loop(lo, hi, send_row, 0)
 
     half = inner // 2
 
@@ -314,16 +310,35 @@
                 acc = acc + dot(hid, dw)
             out[s, n, rows] = acc.astype(BF)
 
-    gate(0, 0)
+    middle(0)
+    to_y.wait_recv()
+    to_x.start()
+    to_core.start()
+    send_two(0, 0, early)
+    for s in range(1, n_seq):
+        send_one(s, early, outer_dev - early)
+    send_two(0, early, outer_dev)
+    loads[6].wait()
+    for c in loads[9:]:
+        c.wait()
+    for n in range(early):
+        gate(0, n)
+    to_x.wait_recv()
+    relay.start()
+    for s in range(1, n_seq):
+        middle(s)
+        send_two(s, 0, outer_dev)
     to_core.wait_recv()
     relay.wait_recv()
+    for n in range(early - 1):
+        feed(0, n)
 
     def step(t, _):
         gate(t // outer_dev, t % outer_dev)
         feed((t - 1) // outer_dev, (t - 1) % outer_dev)
         return 0
 
-    lax.fori_loop(1, n_seq * outer_dev, step, 0)
+    lax.fori_loop(early, n_seq * outer_dev, step, 0)
     feed(n_seq - 1, outer_dev - 1)
 
     for c in direct + passed + [to_y, to_x, to_core, relay]:

time: 124 us -> 121 us (0.976)
  Pallas kernels: 123 us -> 119 us
    pallas_call x1, Pallas kernels: 123 us -> 119 us  [local(): pl.pallas_call(functools.partial(kernel, 1e-06), out_shape=jax.ShapeDtype...]
where the time goes in v3:
time: 121 us
  Pallas kernels  119 us (98%)
  local copies, waits for them, and re-layouts  1.32 us (1%)
    pallas_call x1, Pallas kernels, local(): pl.pallas_call(functools.partial(kernel, 1e-06), out_shape=jax.ShapeDtype...  119 us

profile of v3, /device:TPU:1, one launch (start us, length us, event | category | flops | bytes accessed | tf_op | source)
XLA Modules:
  0.0 120.7 jit_solution(3244865316488648054)
XLA Ops:
  0.0 119.3 %mixer.1 = bf16[2,4,512,256]{3,2,1,0:T(8,128)(2,1)S(1)} custom-call(bf16[2,4,512,256]{3,2,1,0:T(8,128)(2,1)} %bitcast.7, bf16[512,512]{1,0:T(8,128)(2,1)} %fin.1, bf16[128,128]{1,0:T(8,128)(2,1)} %fout.1, f32[4,512]{1,0:T(4,128)} %twf.1, bf16[128,16,256]{2,1,0:T(8,128)(2,1)} %freq.1, bf16[128,128]{1,0:T(8,128)(2,1)} %gout.1, bf16[512,512]{1,0:T(8,128)(2,1)} %gin.1, ...), custom_call_target="tpu_custom_call" | custom-call | tf_op jit(solution)/shard_map/mixer/pallas_call | solution.py:391
  119.4 1.3 %copy.15 = bf16[2,2048,256]{2,1,0:T(8,128)(2,1)} copy(bf16[2,2048,256]{2,1,0:T(8,128)(2,1)S(1)} %bitcast.6) | data formatting | bytes 4194304
